TPU v7x, 32 devices: a whole 2x2x4 slice. The times are simulated.
32 devices in a mesh: ri: 16 (over z, y, core), rj: 2 (over x).
Axes of the slice: x: 2, y: 2, z: 4, core: 2. Of those that a mesh axis runs over, the one named last changes fastest.
Arguments:
- pair: bfloat16 [64, 512, 512], P(None, 'ri', 'rj'), may hold values from -6 to 6
- conv1_weight: bfloat16 [3, 3, 64, 64], replicated, may hold values from -0.25 to 0.25
- conv1_bias: float32 [64], replicated, may hold values from -3 to 3
- conv2_weight: bfloat16 [3, 3, 64, 64], replicated, may hold values from -0.25 to 0.25
- conv2_bias: float32 [64], replicated, may hold values from -3 to 3
- head_weight: bfloat16 [64, 37], replicated, may hold values from -60 to 60, as said below
- head_bias: float32 [37], replicated, may hold values from -4 to 4
- bins: int32 [512, 512], P('ri', 'rj'), may hold values from 0 to 36
- mask: int32 [512], replicated, may hold values from 0 to 1, as said below
Outputs:
- grad_pair: bfloat16 [64, 512, 512], P(None, 'ri', 'rj')
- grad_conv1_weight: float32 [3, 3, 64, 64], replicated
- grad_conv1_bias: float32 [64], replicated
- grad_conv2_weight: float32 [3, 3, 64, 64], replicated
- grad_conv2_bias: float32 [64], replicated
- grad_head_weight: float32 [64, 37], replicated
- grad_head_bias: float32 [37], replicated
Inputs may be any that keep to these rules, and one draw needn't show every extreme that they name: `mask`: residue 0 is always valid; all valid residues lie before some position that is at least 256. `head_weight`: some bins' weights may reach tens in magnitude, so that logits may reach hundreds.
All inputs are finite; a program needn't handle non-finite values.
Results may differ from a plain program's by a relative error of at most 0.012.
The roundings to bfloat16 on the way count: a program that leaves them out, or rounds other values in their place, can miss the bound.
Values may be sent and summed in bfloat16 or wider, within the bound.
A program may use at most 128 MiB of HBM per device.

v0:
```python
import jax
import jax.numpy as jnp
from jax import lax
from jax.sharding import PartitionSpec as P

KERNEL_TAPS = 3
DILATION_RATE = 8


def with_halo(cells, sides, width):
    for axis, dim in sides:
        count = lax.axis_size(axis)
        ends = count - 1
        head = lax.slice_in_dim(cells, 0, width, axis=dim)
        tail = lax.slice_in_dim(cells, cells.shape[dim] - width, cells.shape[dim], axis=dim)
        cells = jnp.concatenate(
            [
                lax.ppermute(tail, axis, [(i, (i + 1) % count) for i in range(ends)]),
                cells,
                lax.ppermute(head, axis, [((i + 1) % count, i) for i in range(ends)]),
            ],
            axis=dim,
        )
    return cells


def activate(value):
    return jnp.where(value > 0, value, jnp.expm1(jnp.minimum(value, 0.0)))


def activate_slope(value):
    return jnp.where(value > 0, 1.0, jnp.exp(jnp.minimum(value, 0.0)))


def with_rims(residual_block):
    return with_halo(residual_block, (("ri", 1), ("rj", 2)), DILATION_RATE * (KERNEL_TAPS // 2))


def dilated(padded_field, weight):
    return lax.conv_general_dilated(
        padded_field[None],
        weight,
        (1, 1),
        [(0, 0), (0, 0)],
        rhs_dilation=(DILATION_RATE, DILATION_RATE),
        dimension_numbers=("NCHW", "HWIO", "NCHW"),
        preferred_element_type=jnp.float32,
    )[0]


def flipped(weight):
    return jnp.transpose(weight[::-1, ::-1], (0, 1, 3, 2))


def tap_sums(padded_field, grad):
    row_extent = grad.shape[1]
    column_extent = grad.shape[2]
    tap_rows = []
    for row_stride in range(KERNEL_TAPS):
        across = []
        for column_stride in range(KERNEL_TAPS):
            sliding_window = padded_field[
                :,
                DILATION_RATE * row_stride : DILATION_RATE * row_stride + row_extent,
                DILATION_RATE * column_stride : DILATION_RATE * column_stride + column_extent,
            ]
            across.append(
                jnp.einsum("cij,dij->cd", sliding_window, grad, preferred_element_type=jnp.float32)
            )
        tap_rows.append(jnp.stack(across))
    return jnp.stack(tap_rows)


def mirror(residual_block, first_move, second_move):
    chan_count, row_count, col_count = residual_block.shape
    col_groups = lax.axis_size("rj")
    row_groups = lax.axis_size("ri") // col_groups
    depth_rows = row_count // col_groups
    sectioned = first_move(residual_block.reshape(chan_count, col_groups, depth_rows, col_count))
    sectioned = sectioned.reshape(chan_count, depth_rows, col_groups * col_count)
    arrived = second_move(sectioned)
    arrived = arrived.reshape(chan_count, row_groups, depth_rows, col_groups, row_count)
    return jnp.transpose(arrived, (0, 4, 1, 3, 2)).reshape(chan_count, row_count, col_count)


def feature_first(sectioned):
    return lax.all_to_all(sectioned, "rj", split_axis=1, concat_axis=3, tiled=True)


def feature_second(sectioned):
    return lax.all_to_all(
        lax.all_to_all(sectioned, "ri", split_axis=2, concat_axis=1, tiled=True),
        "rj",
        split_axis=1,
        concat_axis=2,
        tiled=True,
    )


def slope_first(sectioned):
    return lax.all_to_all(sectioned, "rj", split_axis=1, concat_axis=3, tiled=True)


def slope_second(sectioned):
    return lax.all_to_all(
        lax.all_to_all(sectioned, "ri", split_axis=2, concat_axis=1, tiled=True),
        "rj",
        split_axis=1,
        concat_axis=2,
        tiled=True,
    )


def on_device(
    pair, conv1_weight, conv1_bias, conv2_weight, conv2_bias, head_weight, head_bias, bins, mask
):
    row_count = pair.shape[1]
    col_count = pair.shape[2]
    row_valid = lax.dynamic_slice_in_dim(mask, lax.axis_index("ri") * row_count, row_count).astype(
        jnp.float32
    )
    col_valid = lax.dynamic_slice_in_dim(mask, lax.axis_index("rj") * col_count, col_count).astype(
        jnp.float32
    )
    pair_mask = row_valid[:, None] * col_valid[None, :]
    n_valid = jnp.sum(mask.astype(jnp.float32))
    pair_pad = with_rims(pair)
    inner = dilated(pair_pad, conv1_weight) + conv1_bias[:, None, None]
    inner_act = activate(inner).astype(jnp.bfloat16)
    act_pad = with_rims(inner_act)
    outer = dilated(act_pad, conv2_weight) + conv2_bias[:, None, None]
    summed = pair.astype(jnp.float32) + outer
    hidden = (pair_mask[None] * activate(summed)).astype(jnp.bfloat16)
    mirrored = mirror(hidden, feature_first, feature_second)
    logits = 0.5 * (
        jnp.einsum("ck,cij->kij", head_weight, hidden, preferred_element_type=jnp.float32)
        + jnp.einsum("ck,cij->kij", head_weight, mirrored, preferred_element_type=jnp.float32)
    )
    logits = logits + head_bias[:, None, None]
    peak_logit = jnp.max(logits, axis=0, keepdims=True)
    powered = jnp.exp(logits - peak_logit)
    chance = powered / jnp.sum(powered, axis=0, keepdims=True)
    bin_ids = jnp.arange(head_weight.shape[1], dtype=jnp.int32)[:, None, None]
    onehot = (bins[None, :, :] == bin_ids).astype(jnp.float32)
    error = pair_mask[None] * (chance - onehot)
    symmetric = 0.5 * (hidden.astype(jnp.float32) + mirrored.astype(jnp.float32))
    head_term = jnp.einsum(
        "cij,kij->ck",
        symmetric,
        error,
        precision=lax.Precision.HIGHEST,
        preferred_element_type=jnp.float32,
    )
    head_bias_term = jnp.sum(error, axis=(1, 2))
    weight_wide = head_weight.astype(jnp.float32)
    slope = jnp.einsum(
        "ck,kij->cij",
        weight_wide,
        error,
        precision=lax.Precision.HIGHEST,
        preferred_element_type=jnp.float32,
    )
    slope_mirrored = mirror(slope, slope_first, slope_second)
    half_slope = 0.5 * (slope + slope_mirrored)
    outer_grad = half_slope * pair_mask[None] * activate_slope(summed)
    outer_half = outer_grad.astype(jnp.bfloat16)
    conv2_term = tap_sums(act_pad, outer_half)
    conv2_bias_term = jnp.sum(outer_grad, axis=(1, 2))
    inner_grad = dilated(with_rims(outer_half), flipped(conv2_weight)) * activate_slope(inner)
    inner_half = inner_grad.astype(jnp.bfloat16)
    conv1_term = tap_sums(pair_pad, inner_half)
    conv1_bias_term = jnp.sum(inner_grad, axis=(1, 2))
    grad_pair = (outer_grad + dilated(with_rims(inner_half), flipped(conv1_weight))).astype(
        jnp.bfloat16
    )
    totals = lax.psum(
        (conv1_term, conv1_bias_term, conv2_term, conv2_bias_term, head_term, head_bias_term),
        ("ri", "rj"),
    )
    return (
        grad_pair,
        totals[0] / n_valid,
        totals[1] / n_valid,
        totals[2] / n_valid,
        totals[3] / n_valid,
        totals[4] / n_valid,
        totals[5] / n_valid,
    )


def solution(mesh):
    return jax.shard_map(
        on_device,
        mesh=mesh,
        in_specs=(P(None, "ri", "rj"), P(), P(), P(), P(), P(), P(), P("ri", "rj"), P()),
        out_specs=(P(None, "ri", "rj"), P(), P(), P(), P(), P(), P()),
        check_vma=False,
    )
```

profile of v0, /device:TPU:0, one launch (start us, length us, event | category | flops | bytes accessed | tf_op | source)
XLA Modules:
  0.0 720.4 jit_solution(4406372204763931923)
XLA Ops:
  14.2 2.9 collective-permute-done.1
  18.5 3.4 collective-permute-start.2
  24.5 4.3 collective-permute-done.3
  30.1 3.0 pad_maximum_fusion
  33.1 6.0 copy.145
  39.0 3.2 copy.147
  43.2 3.8 broadcast_select_fusion.3
  50.8 4.6 copy.214
  58.7 5.9 collective-permute-start.4
  86.8 4.5 pad_maximum_fusion.1
  91.3 6.0 copy.154
  97.3 3.2 copy.156
  101.3 3.8 broadcast_select_fusion.2
  108.9 4.6 copy.215
  113.4 3.2 fusion.40
  117.2 16.0 %all_to_all.96 = bf16[64,2,16,256]{3,2,0,1:T(8,128)(2,1)} all-to-all(bf16[64,2,16,256]{3,2,0,1:T(8,128)(2,1)S(1)} %copy.159), channel_id=1, replica_groups=mesh['ri'=16,'rj'=2] {'rj'}, dimensions={1} | all-to-all | bytes 2097152 | tf_op jit(solution)/shard_map/all_to_all | solution.py:87
  133.3 5.1 copy.205
  138.4 4.6 reshape.155
  143.0 37.1 %all_to_all.97 = bf16[16,2,16384]{2,1,0:T(2,128)(2,1)} all-to-all(bf16[16,2,16384]{2,1,0:T(2,128)(2,1)} %reshape.155), channel_id=1, replica_groups=mesh['ri'=16,'rj'=2] {'ri'}, dimensions={0} | all-to-all | bytes 2097152 | tf_op jit(solution)/shard_map/all_to_all | solution.py:92
  180.1 4.7 reshape.156
  184.8 3.5 copy.163
  188.3 3.6 reshape.157
  191.9 4.4 all-to-all-start.2
  196.3 2.7 fusion.114
  199.0 12.2 %all-to-all-done.2 = bf16[2,2,131072]{2,1,0:T(2,128)(2,1)} async-done(((bf16[2,2,131072]{2,1,0:T(2,128)(2,1)}), bf16[2,2,131072]{2,1,0:T(2,128)(2,1)}, u32[]{:S(2)}, u32[]{:S(2)}) %all-to-all-start.2) | async-done | bytes 1048608 | tf_op jit(solution)/shard_map/all_to_all | solution.py:91
  211.2 3.6 reshape.158
  214.8 3.8 copy.165
  218.5 5.1 fusion.153
  223.6 2.7 fusion.111
  227.6 29.0 %all_to_all.98 = f32[64,2,16,256]{3,2,0,1:T(8,128)} all-to-all(f32[64,2,16,256]{3,2,0,1:T(8,128)S(1)} %copy.167), channel_id=1, replica_groups=mesh['ri'=16,'rj'=2] {'rj'}, dimensions={1} | all-to-all | bytes 4194304 | tf_op jit(solution)/shard_map/all_to_all | solution.py:101
  256.6 5.3 copy.208
  261.9 5.5 reshape.159
  267.4 4.4 all-to-all-start.4
  273.1 39.8 %all-to-all-done.4 = f32[16,1,32768]{2,1,0:T(1,128)} async-done(((f32[16,1,32768]{2,1,0:T(1,128)}), f32[16,1,32768]{2,1,0:T(1,128)}, u32[]{:S(2)}, u32[]{:S(2)}) %all-to-all-start.4) | async-done | bytes 2097184 | tf_op jit(solution)/shard_map/all_to_all | solution.py:106
  313.4 8.7 %reduce = f32[16,32768]{1,0:T(8,128)} reduce(f32[16,1,32768]{2,1,0:T(1,128)} %all-to-all-done.4, f32[]{:T(128)} %broadcast.123), dimensions={1}, to_apply=%all_to_all.83.reduce_sub_computation | reduce | bytes 4194308 | tf_op jit(solution)/shard_map/all_to_all | solution.py:106
  322.1 4.2 reshape.160
  326.4 5.5 copy.171
  331.9 5.2 reshape.161
  337.1 4.8 all-to-all-start.5
  341.9 5.1 maximum_maximum_fusion
  347.0 2.7 copy.201
  352.0 4.8 fusion.91
  356.8 11.2 %all-to-all-done.5 = f32[2,1,262144]{2,1,0:T(1,128)} async-done(((f32[2,1,262144]{2,1,0:T(1,128)}), f32[2,1,262144]{2,1,0:T(1,128)}, u32[]{:S(2)}, u32[]{:S(2)}) %all-to-all-start.5) | async-done | bytes 2097184 | tf_op jit(solution)/shard_map/all_to_all | solution.py:105
  368.0 9.5 %reduce.1 = f32[2,262144]{1,0:T(2,128)} reduce(f32[2,1,262144]{2,1,0:T(1,128)} %all-to-all-done.5, f32[]{:T(128)} %broadcast.123), dimensions={1}, to_apply=%all_to_all.87.reduce_sub_computation | reduce | bytes 4194308 | tf_op jit(solution)/shard_map/all_to_all | solution.py:105
  377.5 5.9 reshape.162
  383.4 6.6 copy.173
  390.0 4.2 copy.174
  394.2 5.0 fusion.143
  432.0 4.5 pad_maximum_fusion.2
  436.5 6.0 copy.179
  442.5 3.2 copy.181
  446.4 5.5 broadcast_select_fusion.1
  455.8 4.7 copy.216
  460.5 3.5 fusion.139
  474.1 5.2 collective-permute-start.12
  480.6 48.6 %all-reduce = (f32[64]{0:T(128)S(1)}, f32[64]{0:T(128)S(1)}, f32[64,37]{0,1:T(8,128)S(1)}, f32[37]{0:T(128)}) all-reduce(f32[64]{0:T(128)} %get-tuple-element.43, f32[64]{0:T(128)} %get-tuple-element.41, f32[64,37]{0,1:T(8,128)} %fusion.91, f32[37]{0:T(128)} %fusion.142), channel_id=1, replica_groups=mesh['ri'=16,'rj'=2] {'ri','rj'}, use_global_device_ids=true, to_apply=%region_5.6 | all-reduce | flops 2533 | bytes 20264 | tf_op jit(solution)/shard_map/psum | solution.py:176
  536.9 126.6 %all-reduce.4.cloned.1.call-done = (f32[3,3,64,64]{3,2,1,0:T(8,128)}, f32[3,3,64,64]{3,2,1,0:T(8,128)}) async-done(((f32[3,3,64,64]{3,2,1,0:T(8,128)}, f32[3,3,64,64]{3,2,1,0:T(8,128)}), (f32[3,3,64,64]{3,2,1,0:T(8,128)}, f32[3,3,64,64]{3,2,1,0:T(8,128)})) %all-reduce.4.cloned.1.call-update) | async-done | bytes 294928 | tf_op jit(solution)/shard_map/psum | solution.py:176
  670.1 3.4 collective-permute-start.14
  677.7 2.7 collective-permute-done.15
  680.7 4.5 pad_maximum_fusion.3
  685.2 6.0 copy.188
  691.2 3.2 copy.190
  695.3 5.5 broadcast_select_fusion
  704.7 4.5 copy.217
  (173 shorter events, 129.0 us)
Async XLA Ops:
  7.2 93.9 %copy-start = (bf16[3,3,64,64]{3,2,1,0:T(8,128)(2,1)S(1)}, bf16[3,3,64,64]{3,2,1,0:T(8,128)(2,1)}, u32[]{:S(2)}) copy-start(bf16[3,3,64,64]{3,2,1,0:T(8,128)(2,1)} %param.12) | copy-start | bytes 221188
  7.2 6.4 copy-start.4
  9.1 3.7 copy-start.10
  9.2 3.7 collective-permute-start
  11.5 5.5 collective-permute-start.1
  12.9 0.7 copy-start.18
  17.1 0.7 copy-start.20
  18.5 5.6 collective-permute-start.2
  22.2 6.6 collective-permute-start.3
  30.1 3.0 copy-start.8
  42.3 0.9 copy-start.25
  42.3 0.9 copy-start.27
  58.7 10.0 %collective-permute-start.4 = (bf16[64,8,256]{2,0,1:T(8,128)(2,1)}, bf16[64,8,256]{2,0,1:T(8,128)(2,1)}, u32[]{:S(2)}, u32[]{:S(2)}) collective-permute-start(bf16[64,8,256]{2,0,1:T(8,128)(2,1)} %get-tuple-element.59), channel_id=1, source_target_pairs={{0,2},{2,4},{4,6},{6,8},{8,10},{10,12},{12,14},{14,16},{16,18},{18... | collective-permute-start | bytes 786440 | tf_op jit(solution)/shard_map/ppermute | solution.py:18
  64.7 4.1 collective-permute-start.5
  73.6 7.0 collective-permute-start.6
  78.0 6.8 collective-permute-start.7
  100.6 0.7 copy-start.28
  116.6 16.6 %copy-start.6 = (bf16[64,32,256]{2,0,1:T(8,128)(2,1)}, bf16[64,32,256]{2,0,1:T(8,128)(2,1)S(1)}, u32[]{:S(2)}) copy-start(bf16[64,32,256]{2,0,1:T(8,128)(2,1)S(1)} %fusion.40) | copy-start | bytes 3145732
  191.9 19.3 %all-to-all-start.2 = ((bf16[2,2,131072]{2,1,0:T(2,128)(2,1)}), bf16[2,2,131072]{2,1,0:T(2,128)(2,1)}, u32[]{:S(2)}, u32[]{:S(2)}) async-start(bf16[2,2,131072]{2,1,0:T(2,128)(2,1)} %reshape.157), calls=%async_computation.2 | async-start | bytes 2097152 | tf_op jit(solution)/shard_map/all_to_all | solution.py:91
  226.3 1.3 copy-start.7
  267.4 45.5 %all-to-all-start.4 = ((f32[16,1,32768]{2,1,0:T(1,128)}), f32[16,1,32768]{2,1,0:T(1,128)}, u32[]{:S(2)}, u32[]{:S(2)}) async-start(f32[16,1,32768]{2,1,0:T(1,128)} %reshape.159), calls=%async_computation.4 | async-start | bytes 4194304 | tf_op jit(solution)/shard_map/all_to_all | solution.py:106
  337.1 31.0 %all-to-all-start.5 = ((f32[2,1,262144]{2,1,0:T(1,128)}), f32[2,1,262144]{2,1,0:T(1,128)}, u32[]{:S(2)}, u32[]{:S(2)}) async-start(f32[2,1,262144]{2,1,0:T(1,128)} %reshape.161), calls=%async_computation.5 | async-start | bytes 4194304 | tf_op jit(solution)/shard_map/all_to_all | solution.py:105
  341.9 321.6 %all-reduce.4.cloned.1.call-start = ((), (), s32[]{:S(2)}) async-start(), calls=%async_computation.6 | async-start | bytes 1179648 | tf_op jit(solution)/shard_map/psum | solution.py:176
  399.2 1.3 copy-start.3
  399.2 2.8 copy-start.13
  399.3 15.2 %copy-start.1 = (bf16[64,32,256]{2,0,1:T(8,128)(2,1)}, bf16[64,32,256]{2,0,1:T(8,128)(2,1)S(1)}, u32[]{:S(2)}) copy-start(bf16[64,32,256]{2,0,1:T(8,128)(2,1)S(1)} %convert_element_type.43) | copy-start | bytes 3145732
  402.0 1.7 copy-start.12
  406.2 7.3 %collective-permute-start.8 = (bf16[64,8,256]{2,0,1:T(8,128)(2,1)S(1)}, bf16[64,8,256]{2,0,1:T(8,128)(2,1)S(1)}, u32[]{:S(2)}, u32[]{:S(2)}) collective-permute-start(bf16[64,8,256]{2,0,1:T(8,128)(2,1)S(1)} %get-tuple-element.57), channel_id=1, source_target_pairs={{0,2},{2,4},{4,6},{6,8},{8,10},{10,12},{12,14},{14,16},{16,18},{18... | collective-permute-start | bytes 786440 | tf_op jit(solution)/shard_map/ppermute | solution.py:18
  408.0 6.5 collective-permute-start.9
  413.4 2.9 copy-start.16
  414.5 1.8 copy-start.17
  416.3 15.7 %copy-start.2 = (bf16[64,32,256]{2,0,1:T(8,128)(2,1)S(1)}, bf16[64,32,256]{2,0,1:T(8,128)(2,1)}, u32[]{:S(2)}) copy-start(bf16[64,32,256]{2,0,1:T(8,128)(2,1)} %copy-done.1) | copy-start | bytes 3145732
  418.4 7.7 %collective-permute-start.10 = (bf16[64,48,8]{0,2,1:T(8,128)(2,1)}, bf16[64,48,8]{0,2,1:T(8,128)(2,1)}, u32[]{:S(2)}, u32[]{:S(2)}) collective-permute-start(bf16[64,48,8]{0,2,1:T(8,128)(2,1)} %copy.175), channel_id=1, source_target_pairs={{0,1},{2,3},{4,5},{6,7},{8,9},{10,11},{12,13},{14,15},{16,17},{18,... | collective-permute-start | bytes 147464 | tf_op jit(solution)/shard_map/ppermute | solution.py:18
  423.1 6.8 collective-permute-start.11
  445.7 0.7 copy-start.29
  464.1 1.2 copy-start.9
  465.2 1.3 copy-start.5
  473.3 60.7 %copy-start.11 = (bf16[64,32,256]{2,0,1:T(8,128)(2,1)S(1)}, bf16[64,32,256]{2,0,1:T(8,128)(2,1)}, u32[]{:S(2)}) copy-start(bf16[64,32,256]{2,0,1:T(8,128)(2,1)} %copy-done.10) | copy-start | bytes 3145732
  473.3 60.7 %copy-start.19 = (bf16[64,8,256]{2,0,1:T(8,128)(2,1)S(1)}, bf16[64,8,256]{2,0,1:T(8,128)(2,1)}, u32[]{:S(2)}) copy-start(bf16[64,8,256]{2,0,1:T(8,128)(2,1)} %copy-done.18) | copy-start | bytes 786436
  474.1 191.7 %collective-permute-start.12 = (bf16[64,8,256]{2,0,1:T(8,128)(2,1)}, bf16[64,8,256]{2,0,1:T(8,128)(2,1)S(1)}, u32[]{:S(2)}, u32[]{:S(2)}) collective-permute-start(bf16[64,8,256]{2,0,1:T(8,128)(2,1)} %get-tuple-element.55), channel_id=1, source_target_pairs={{0,2},{2,4},{4,6},{6,8},{8,10},{10,12},{12,14},{14,16},{16,18},{18... | collective-permute-start | bytes 786440 | tf_op jit(solution)/shard_map/ppermute | solution.py:18
  479.3 186.5 %collective-permute-start.13 = (bf16[64,8,256]{2,0,1:T(8,128)(2,1)S(1)}, bf16[64,8,256]{2,0,1:T(8,128)(2,1)S(1)}, u32[]{:S(2)}, u32[]{:S(2)}) collective-permute-start(bf16[64,8,256]{2,0,1:T(8,128)(2,1)S(1)} %get-tuple-element.56), channel_id=1, source_target_pairs={{2,0},{4,2},{6,4},{8,6},{10,8},{12,10},{14,12},{16,14},{18,16},{20... | collective-permute-start | bytes 786440 | tf_op jit(solution)/shard_map/ppermute | solution.py:20
  532.3 2.1 copy-start.21
  532.3 2.1 copy-start.22
  532.3 2.1 copy-start.23
  532.3 2.1 copy-start.24
  665.8 0.7 copy-start.14
  666.5 0.7 copy-start.15
  670.1 7.2 %collective-permute-start.14 = (bf16[64,48,8]{0,2,1:T(8,128)(2,1)S(1)}, bf16[64,48,8]{0,2,1:T(8,128)(2,1)S(1)}, u32[]{:S(2)}, u32[]{:S(2)}) collective-permute-start(bf16[64,48,8]{0,2,1:T(8,128)(2,1)S(1)} %copy.184), channel_id=1, source_target_pairs={{0,1},{2,3},{4,5},{6,7},{8,9},{10,11},{12,13},{14,15},{16,17},{18,... | collective-permute-start | bytes 147464 | tf_op jit(solution)/shard_map/ppermute | solution.py:18
  673.7 6.6 collective-permute-start.15
  694.4 0.9 copy-start.26
  694.4 0.9 copy-start.30
Sparse Core Ops, SparseCore 0:
  535.4 128.0 all-reduce.3
where the time goes:
time: 726 us; the launch traced here: 720 us
  waiting for transfers between devices  205 us (28%)
  local copies, waits for them, and re-layouts  188 us (26%)
  blocking collectives  131 us (18%)
  other arithmetic  78.8 us (11%)
  starting transfers between devices  51.8 us (7%)
  matrix products  51.3 us (7%)
  between operations  15 us (2%)
    psum x1, waiting for transfers between devices, on_device(): lax.psum((conv1_term, conv1_bias_term, conv2_term, conv2_bias_term, head_...  127 us
    unnamed x78, local copies, waits for them, and re-layouts  67.4 us
    psum x1, blocking collectives, on_device(): lax.psum((conv1_term, conv1_bias_term, conv2_term, conv2_bias_term, head_...  48.6 us
    all_to_all x1, waiting for transfers between devices, slope_second(): lax.all_to_all(sectioned, 'ri', split_axis=2, concat_axis=1, tiled=True)  39.8 us
    all_to_all x1, blocking collectives, feature_second(): lax.all_to_all(sectioned, 'ri', split_axis=2, concat_axis=1, tiled=True)  37.1 us
    conv_general_dilated x16, local copies, waits for them, and re-layouts, dilated(): lax.conv_general_dilated(padded_field[None], weight, (1, 1), [(0, 0), (0,...  30.2 us
    all_to_all x1, blocking collectives, slope_first(): lax.all_to_all(sectioned, 'rj', split_axis=1, concat_axis=3, tiled=True)  29 us
    ppermute x8, starting transfers between devices, with_halo(): lax.ppermute(tail, axis, [(i, (i + 1) % count) for i in range(ends)])  27.1 us
  transfers between devices with their start and end apart: 20, of which 11 were waited for; matrix products, arithmetic and copies ran while one was open for 7% of the time, Pallas kernels for 0%

commit v1 on v0

--- a/solution.py
+++ b/solution.py
@@ -2,6 +2,7 @@
 import jax.numpy as jnp
 from jax import lax
 from jax.sharding import PartitionSpec as P
+from jax.lax import psum
 
 KERNEL_TAPS = 3
 DILATION_RATE = 8
@@ -173,10 +174,11 @@
     grad_pair = (outer_grad + dilated(with_rims(inner_half), flipped(conv1_weight))).astype(
         jnp.bfloat16
     )
-    totals = lax.psum(
+    f_now = psum(
         (conv1_term, conv1_bias_term, conv2_term, conv2_bias_term, head_term, head_bias_term),
-        ("ri", "rj"),
-    )
+        axis_name="rj",
+    )
+    totals = psum(f_now, axis_name="ri")
     return (
         grad_pair,
         totals[0] / n_valid,

time: 726 us -> 671 us (0.924)
  waiting for transfers between devices: 205 us -> 132 us
  blocking collectives: 131 us -> 154 us
    psum x1 -> x2, waiting for transfers between devices: 127 us -> 54 us  [the longest x1 54 us: on_device(): totals = psum(f_now, axis_name='ri')]
    psum x1 -> x2, blocking collectives: 48.6 us -> 72.2 us  [the longest x1 63 us: on_device(): totals = psum(f_now, axis_name='ri')]
    unnamed x78 -> x80, local copies, waits for them, and re-layouts: 67.4 us -> 68.6 us
  transfers between devices with their start and end apart: 20 -> 21, of which waited for: 11 -> 11; matrix products, arithmetic and copies ran while one was open for 7% -> 12% of each run, Pallas kernels for 0% -> 0%
where the time goes in v1:
time: 671 us; the launch traced here: 665 us
  local copies, waits for them, and re-layouts  189 us (28%)
  blocking collectives  154 us (23%)
  waiting for transfers between devices  132 us (20%)
  other arithmetic  78.1 us (12%)
  starting transfers between devices  50.9 us (8%)
  matrix products  45.7 us (7%)
  between operations  15.1 us (2%)
    unnamed x80, local copies, waits for them, and re-layouts  68.6 us
    psum x1, blocking collectives, on_device(): totals = psum(f_now, axis_name='ri')  63 us
    psum x1, waiting for transfers between devices, on_device(): totals = psum(f_now, axis_name='ri')  54 us
    all_to_all x1, waiting for transfers between devices, slope_second(): lax.all_to_all(sectioned, 'ri', split_axis=2, concat_axis=1, tiled=True)  39.8 us
    all_to_all x1, blocking collectives, feature_second(): lax.all_to_all(sectioned, 'ri', split_axis=2, concat_axis=1, tiled=True)  37.1 us
    conv_general_dilated x16, local copies, waits for them, and re-layouts, dilated(): lax.conv_general_dilated(padded_field[None], weight, (1, 1), [(0, 0), (0,...  30.2 us
    all_to_all x1, blocking collectives, slope_first(): lax.all_to_all(sectioned, 'rj', split_axis=1, concat_axis=3, tiled=True)  29 us
    ppermute x8, starting transfers between devices, with_halo(): lax.ppermute(tail, axis, [(i, (i + 1) % count) for i in range(ends)])  26.2 us
  transfers between devices with their start and end apart: 21, of which 11 were waited for; matrix products, arithmetic and copies ran while one was open for 12% of the time, Pallas kernels for 0%

profile of v1, /device:TPU:0, one launch (start us, length us, event | category | flops | bytes accessed | tf_op | source)
XLA Modules:
  0.0 665.1 jit_solution(9913654682579900262)
XLA Ops:
  14.2 2.9 collective-permute-done.1
  18.5 3.4 collective-permute-start.2
  24.5 4.3 collective-permute-done.3
  30.1 3.0 pad_maximum_fusion
  33.1 6.0 copy.145
  39.0 3.2 copy.147
  43.2 3.8 broadcast_select_fusion.3
  50.8 4.6 copy.214
  58.7 6.0 collective-permute-start.4
  86.9 4.4 pad_maximum_fusion.1
  91.3 6.0 copy.154
  97.2 3.2 copy.156
  101.2 3.8 broadcast_select_fusion.2
  108.8 4.6 copy.215
  113.3 3.2 fusion.40
  117.1 16.1 %all_to_all.96 = bf16[64,2,16,256]{3,2,0,1:T(8,128)(2,1)} all-to-all(bf16[64,2,16,256]{3,2,0,1:T(8,128)(2,1)S(1)} %copy.159), channel_id=1, replica_groups=mesh['ri'=16,'rj'=2] {'rj'}, dimensions={1} | all-to-all | bytes 2097152 | tf_op jit(solution)/shard_map/all_to_all | solution.py:88
  133.2 5.1 copy.205
  138.3 4.6 reshape.155
  142.9 37.1 %all_to_all.97 = bf16[16,2,16384]{2,1,0:T(2,128)(2,1)} all-to-all(bf16[16,2,16384]{2,1,0:T(2,128)(2,1)} %reshape.155), channel_id=1, replica_groups=mesh['ri'=16,'rj'=2] {'ri'}, dimensions={0} | all-to-all | bytes 2097152 | tf_op jit(solution)/shard_map/all_to_all | solution.py:93
  180.0 4.7 reshape.156
  184.7 3.5 copy.163
  188.2 3.6 reshape.157
  191.8 4.4 all-to-all-start.2
  198.9 12.2 %all-to-all-done.2 = bf16[2,2,131072]{2,1,0:T(2,128)(2,1)} async-done(((bf16[2,2,131072]{2,1,0:T(2,128)(2,1)}), bf16[2,2,131072]{2,1,0:T(2,128)(2,1)}, u32[]{:S(2)}, u32[]{:S(2)}) %all-to-all-start.2) | async-done | bytes 1048608 | tf_op jit(solution)/shard_map/all_to_all | solution.py:92
  211.1 3.6 reshape.158
  214.7 3.8 copy.165
  218.4 5.1 fusion.153
  223.5 2.7 fusion.111
  227.6 29.0 %all_to_all.98 = f32[64,2,16,256]{3,2,0,1:T(8,128)} all-to-all(f32[64,2,16,256]{3,2,0,1:T(8,128)S(1)} %copy.167), channel_id=1, replica_groups=mesh['ri'=16,'rj'=2] {'rj'}, dimensions={1} | all-to-all | bytes 4194304 | tf_op jit(solution)/shard_map/all_to_all | solution.py:102
  256.6 5.3 copy.208
  261.8 5.5 reshape.159
  267.3 4.4 all-to-all-start.4
  273.1 39.8 %all-to-all-done.4 = f32[16,1,32768]{2,1,0:T(1,128)} async-done(((f32[16,1,32768]{2,1,0:T(1,128)}), f32[16,1,32768]{2,1,0:T(1,128)}, u32[]{:S(2)}, u32[]{:S(2)}) %all-to-all-start.4) | async-done | bytes 2097184 | tf_op jit(solution)/shard_map/all_to_all | solution.py:107
  313.4 8.7 %reduce = f32[16,32768]{1,0:T(8,128)} reduce(f32[16,1,32768]{2,1,0:T(1,128)} %all-to-all-done.4, f32[]{:T(128)} %broadcast.123), dimensions={1}, to_apply=%all_to_all.83.reduce_sub_computation | reduce | bytes 4194308 | tf_op jit(solution)/shard_map/all_to_all | solution.py:107
  322.0 4.2 reshape.160
  326.3 5.5 copy.171
  331.8 5.2 reshape.161
  337.0 4.8 all-to-all-start.5
  341.9 5.1 maximum_maximum_fusion
  347.0 2.7 copy.201
  352.0 4.8 fusion.91
  356.8 11.2 %all-to-all-done.5 = f32[2,1,262144]{2,1,0:T(1,128)} async-done(((f32[2,1,262144]{2,1,0:T(1,128)}), f32[2,1,262144]{2,1,0:T(1,128)}, u32[]{:S(2)}, u32[]{:S(2)}) %all-to-all-start.5) | async-done | bytes 2097184 | tf_op jit(solution)/shard_map/all_to_all | solution.py:106
  368.0 9.5 %reduce.1 = f32[2,262144]{1,0:T(2,128)} reduce(f32[2,1,262144]{2,1,0:T(1,128)} %all-to-all-done.5, f32[]{:T(128)} %broadcast.123), dimensions={1}, to_apply=%all_to_all.87.reduce_sub_computation | reduce | bytes 4194308 | tf_op jit(solution)/shard_map/all_to_all | solution.py:106
  377.4 5.8 reshape.162
  383.3 6.6 copy.173
  389.9 4.2 copy.174
  394.1 5.0 fusion.143
  418.3 2.7 collective-permute-start.10
  431.9 4.4 pad_maximum_fusion.2
  436.3 6.0 copy.179
  442.3 3.2 copy.181
  446.2 5.5 broadcast_select_fusion.1
  455.6 4.7 copy.216
  460.3 3.5 fusion.139
  470.0 5.4 collective-permute-start.12
  478.5 9.2 %all-reduce.2 = (f32[64]{0:T(128)S(1)}, f32[64]{0:T(128)S(1)}, f32[64,37]{0,1:T(8,128)S(1)}, f32[37]{0:T(128)S(1)}) all-reduce(f32[64]{0:T(128)S(1)} %copy-done.25, f32[64]{0:T(128)S(1)} %copy-done.24, f32[64,37]{0,1:T(8,128)S(1)} %copy-done.22, f32[37]{0:T(128)S(1)} %copy-done.23), channel_id=1, replica_groups=mesh['ri'=16,'rj'=2] {'rj'}, use_global_device_ids=true, to_apply=%region_6.7 | all-reduce | flops 2533 | bytes 20264 | tf_op jit(solution)/shard_map/psum | solution.py:177
  487.8 63.0 %all-reduce = (f32[64]{0:T(128)S(1)}, f32[64]{0:T(128)S(1)}, f32[64,37]{0,1:T(8,128)S(1)}, f32[37]{0:T(128)}) all-reduce(f32[64]{0:T(128)S(1)} %get-tuple-element.41, f32[64]{0:T(128)S(1)} %get-tuple-element.42, f32[64,37]{0,1:T(8,128)S(1)} %get-tuple-element.43, f32[37]{0:T(128)S(1)} %get-tuple-element.44), channel_id=1, replica_groups=mesh['ri'=16,'rj'=2] {'ri'}, use_global_device_ids=true, to_apply=%region_7.8 | all-reduce | flops 2533 | bytes 20264 | tf_op jit(solution)/shard_map/psum | solution.py:181
  563.5 3.0 collective-permute-done.15
  566.9 4.4 pad_maximum_fusion.3
  571.3 6.0 copy.188
  577.2 3.3 copy.190
  581.4 5.5 broadcast_select_fusion
  590.8 4.5 copy.217
  599.4 54.0 %all-reduce.7.cloned.1.call-done = (f32[3,3,64,64]{3,2,1,0:T(8,128)}, f32[3,3,64,64]{3,2,1,0:T(8,128)}) async-done(((f32[3,3,64,64]{3,2,1,0:T(8,128)}, f32[3,3,64,64]{3,2,1,0:T(8,128)}), (f32[3,3,64,64]{3,2,1,0:T(8,128)}, f32[3,3,64,64]{3,2,1,0:T(8,128)})) %all-reduce.7.cloned.1.call-update) | async-done | bytes 294928 | tf_op jit(solution)/shard_map/psum | solution.py:181
  (179 shorter events, 125.8 us)
Async XLA Ops:
  7.2 93.8 %copy-start = (bf16[3,3,64,64]{3,2,1,0:T(8,128)(2,1)S(1)}, bf16[3,3,64,64]{3,2,1,0:T(8,128)(2,1)}, u32[]{:S(2)}) copy-start(bf16[3,3,64,64]{3,2,1,0:T(8,128)(2,1)} %param.12) | copy-start | bytes 221188
  7.2 6.4 copy-start.4
  9.1 3.7 copy-start.10
  9.2 3.7 collective-permute-start
  11.5 5.5 collective-permute-start.1
  12.9 0.7 copy-start.18
  17.1 0.7 copy-start.20
  18.5 5.6 collective-permute-start.2
  22.2 6.6 collective-permute-start.3
  30.1 3.0 copy-start.8
  42.3 0.9 copy-start.26
  42.3 0.9 copy-start.28
  58.7 10.0 %collective-permute-start.4 = (bf16[64,8,256]{2,0,1:T(8,128)(2,1)}, bf16[64,8,256]{2,0,1:T(8,128)(2,1)}, u32[]{:S(2)}, u32[]{:S(2)}) collective-permute-start(bf16[64,8,256]{2,0,1:T(8,128)(2,1)} %get-tuple-element.65), channel_id=1, source_target_pairs={{0,2},{2,4},{4,6},{6,8},{8,10},{10,12},{12,14},{14,16},{16,18},{18... | collective-permute-start | bytes 786440 | tf_op jit(solution)/shard_map/ppermute | solution.py:19
  64.7 4.1 collective-permute-start.5
  73.6 7.1 %collective-permute-start.6 = (bf16[64,48,8]{0,2,1:T(8,128)(2,1)}, bf16[64,48,8]{0,2,1:T(8,128)(2,1)}, u32[]{:S(2)}, u32[]{:S(2)}) collective-permute-start(bf16[64,48,8]{0,2,1:T(8,128)(2,1)} %copy.150), channel_id=1, source_target_pairs={{0,1},{2,3},{4,5},{6,7},{8,9},{10,11},{12,13},{14,15},{16,17},{18,... | collective-permute-start | bytes 147464 | tf_op jit(solution)/shard_map/ppermute | solution.py:19
  78.0 6.8 %collective-permute-start.7 = (bf16[64,48,8]{0,2,1:T(8,128)(2,1)}, bf16[64,48,8]{0,2,1:T(8,128)(2,1)}, u32[]{:S(2)}, u32[]{:S(2)}) collective-permute-start(bf16[64,48,8]{0,2,1:T(8,128)(2,1)} %copy.151), channel_id=1, source_target_pairs={{1,0},{3,2},{5,4},{7,6},{9,8},{11,10},{13,12},{15,14},{17,16},{19,... | collective-permute-start | bytes 147464 | tf_op jit(solution)/shard_map/ppermute | solution.py:21
  100.5 0.7 copy-start.29
  116.5 16.7 %copy-start.6 = (bf16[64,32,256]{2,0,1:T(8,128)(2,1)}, bf16[64,32,256]{2,0,1:T(8,128)(2,1)S(1)}, u32[]{:S(2)}) copy-start(bf16[64,32,256]{2,0,1:T(8,128)(2,1)S(1)} %fusion.40) | copy-start | bytes 3145732
  191.8 19.3 %all-to-all-start.2 = ((bf16[2,2,131072]{2,1,0:T(2,128)(2,1)}), bf16[2,2,131072]{2,1,0:T(2,128)(2,1)}, u32[]{:S(2)}, u32[]{:S(2)}) async-start(bf16[2,2,131072]{2,1,0:T(2,128)(2,1)} %reshape.157), calls=%async_computation.2 | async-start | bytes 2097152 | tf_op jit(solution)/shard_map/all_to_all | solution.py:92
  226.2 1.3 copy-start.7
  267.3 45.5 %all-to-all-start.4 = ((f32[16,1,32768]{2,1,0:T(1,128)}), f32[16,1,32768]{2,1,0:T(1,128)}, u32[]{:S(2)}, u32[]{:S(2)}) async-start(f32[16,1,32768]{2,1,0:T(1,128)} %reshape.159), calls=%async_computation.4 | async-start | bytes 4194304 | tf_op jit(solution)/shard_map/all_to_all | solution.py:107
  337.0 31.0 %all-to-all-start.5 = ((f32[2,1,262144]{2,1,0:T(1,128)}), f32[2,1,262144]{2,1,0:T(1,128)}, u32[]{:S(2)}, u32[]{:S(2)}) async-start(f32[2,1,262144]{2,1,0:T(1,128)} %reshape.161), calls=%async_computation.5 | async-start | bytes 4194304 | tf_op jit(solution)/shard_map/all_to_all | solution.py:106
  341.8 221.3 %all-reduce.9.cloned.1.call-start = ((), (), s32[]{:S(2)}) async-start(), calls=%async_computation.7 | async-start | bytes 1179648 | tf_op jit(solution)/shard_map/psum | solution.py:177
  399.1 1.3 copy-start.3
  399.1 2.8 copy-start.13
  399.2 15.2 %copy-start.1 = (bf16[64,32,256]{2,0,1:T(8,128)(2,1)}, bf16[64,32,256]{2,0,1:T(8,128)(2,1)S(1)}, u32[]{:S(2)}) copy-start(bf16[64,32,256]{2,0,1:T(8,128)(2,1)S(1)} %convert_element_type.43) | copy-start | bytes 3145732
  401.9 1.7 copy-start.12
  406.1 7.3 %collective-permute-start.8 = (bf16[64,8,256]{2,0,1:T(8,128)(2,1)S(1)}, bf16[64,8,256]{2,0,1:T(8,128)(2,1)S(1)}, u32[]{:S(2)}, u32[]{:S(2)}) collective-permute-start(bf16[64,8,256]{2,0,1:T(8,128)(2,1)S(1)} %get-tuple-element.63), channel_id=1, source_target_pairs={{0,2},{2,4},{4,6},{6,8},{8,10},{10,12},{12,14},{14,16},{16,18},{18... | collective-permute-start | bytes 786440 | tf_op jit(solution)/shard_map/ppermute | solution.py:19
  407.9 6.5 collective-permute-start.9
  413.3 2.9 copy-start.16
  414.4 1.8 copy-start.17
  416.2 15.7 %copy-start.2 = (bf16[64,32,256]{2,0,1:T(8,128)(2,1)S(1)}, bf16[64,32,256]{2,0,1:T(8,128)(2,1)}, u32[]{:S(2)}) copy-start(bf16[64,32,256]{2,0,1:T(8,128)(2,1)} %copy-done.1) | copy-start | bytes 3145732
  418.3 7.7 %collective-permute-start.10 = (bf16[64,48,8]{0,2,1:T(8,128)(2,1)}, bf16[64,48,8]{0,2,1:T(8,128)(2,1)}, u32[]{:S(2)}, u32[]{:S(2)}) collective-permute-start(bf16[64,48,8]{0,2,1:T(8,128)(2,1)} %copy.175), channel_id=1, source_target_pairs={{0,1},{2,3},{4,5},{6,7},{8,9},{10,11},{12,13},{14,15},{16,17},{18,... | collective-permute-start | bytes 147464 | tf_op jit(solution)/shard_map/ppermute | solution.py:19
  423.1 6.8 %collective-permute-start.11 = (bf16[64,48,8]{0,2,1:T(8,128)(2,1)}, bf16[64,48,8]{0,2,1:T(8,128)(2,1)}, u32[]{:S(2)}, u32[]{:S(2)}) collective-permute-start(bf16[64,48,8]{0,2,1:T(8,128)(2,1)} %copy.176), channel_id=1, source_target_pairs={{1,0},{3,2},{5,4},{7,6},{9,8},{11,10},{13,12},{15,14},{17,16},{19,... | collective-permute-start | bytes 147464 | tf_op jit(solution)/shard_map/ppermute | solution.py:21
  445.5 0.7 copy-start.30
  463.8 1.1 copy-start.9
  465.0 1.2 copy-start.5
  469.4 7.3 %copy-start.11 = (bf16[64,32,256]{2,0,1:T(8,128)(2,1)S(1)}, bf16[64,32,256]{2,0,1:T(8,128)(2,1)}, u32[]{:S(2)}) copy-start(bf16[64,32,256]{2,0,1:T(8,128)(2,1)} %copy-done.10) | copy-start | bytes 3145732
  469.4 7.3 %copy-start.21 = (bf16[64,8,256]{2,0,1:T(8,128)(2,1)S(1)}, bf16[64,8,256]{2,0,1:T(8,128)(2,1)}, u32[]{:S(2)}) copy-start(bf16[64,8,256]{2,0,1:T(8,128)(2,1)} %copy-done.20) | copy-start | bytes 786436
  470.0 7.2 %copy-start.19 = (bf16[64,8,256]{2,0,1:T(8,128)(2,1)S(1)}, bf16[64,8,256]{2,0,1:T(8,128)(2,1)}, u32[]{:S(2)}) copy-start(bf16[64,8,256]{2,0,1:T(8,128)(2,1)} %copy-done.18) | copy-start | bytes 786436
  470.0 83.1 %collective-permute-start.12 = (bf16[64,8,256]{2,0,1:T(8,128)(2,1)S(1)}, bf16[64,8,256]{2,0,1:T(8,128)(2,1)S(1)}, u32[]{:S(2)}, u32[]{:S(2)}) collective-permute-start(bf16[64,8,256]{2,0,1:T(8,128)(2,1)S(1)} %get-tuple-element.61), channel_id=1, source_target_pairs={{0,2},{2,4},{4,6},{6,8},{8,10},{10,12},{12,14},{14,16},{16,18},{18... | collective-permute-start | bytes 786440 | tf_op jit(solution)/shard_map/ppermute | solution.py:19
  475.4 77.8 %collective-permute-start.13 = (bf16[64,8,256]{2,0,1:T(8,128)(2,1)S(1)}, bf16[64,8,256]{2,0,1:T(8,128)(2,1)S(1)}, u32[]{:S(2)}, u32[]{:S(2)}) collective-permute-start(bf16[64,8,256]{2,0,1:T(8,128)(2,1)S(1)} %get-tuple-element.62), channel_id=1, source_target_pairs={{2,0},{4,2},{6,4},{8,6},{10,8},{12,10},{14,12},{16,14},{18,16},{20... | collective-permute-start | bytes 786440 | tf_op jit(solution)/shard_map/ppermute | solution.py:21
  477.2 1.3 copy-start.22
  477.2 1.3 copy-start.23
  477.2 1.3 copy-start.24
  477.2 1.3 copy-start.25
  478.4 175.0 %all-reduce.7.cloned.1.call-start = ((), (), s32[]{:S(2)}) async-start(), calls=%async_computation.6 | async-start | bytes 1179648 | tf_op jit(solution)/shard_map/psum | solution.py:181
  553.2 0.7 copy-start.14
  553.9 0.8 copy-start.15
  557.5 5.6 collective-permute-start.14
  560.0 6.5 collective-permute-start.15
  580.5 0.9 copy-start.27
  580.5 0.9 copy-start.31
Sparse Core Ops, SparseCore 0:
  478.6 37.5 all-reduce.8
  563.3 90.1 all-reduce.6
